TPU v7x, 32 devices: a whole 2x2x4 slice. The times are simulated.
32 devices in a mesh: tm: 8 (over z, y), chan: 4 (over x, core).
Axes of the slice: x: 2, y: 2, z: 4, core: 2. Of those that a mesh axis runs over, the one named last changes fastest.
Arguments:
- tokens: bfloat16 [16384, 1024], P('tm', 'chan'), may hold values from -170 to 170
- w_query: bfloat16 [1024, 1024], P(None, 'chan'), may hold values from -0.1875 to 0.1875
- w_key: bfloat16 [1024, 1024], P(None, 'chan'), may hold values from -0.1875 to 0.1875
- w_value: bfloat16 [1024, 1024], P(None, 'chan'), may hold values from -0.1875 to 0.1875
- w_out: bfloat16 [1024, 1024], P('chan'), may hold values from -0.25 to 0.25
- pool_kernel: float32 [2, 27, 64], replicated, may hold values from -1.25 to 1.25
Outputs:
- block_out: bfloat16 [16384, 1024], P('tm', 'chan')
All inputs are finite; a program needn't handle non-finite values.
Results may differ from a plain program's by a relative error of at most 0.0053.
Values may be sent and summed in bfloat16 or wider, within the bound.
A program may use at most 128 MiB of HBM per device.

v0:
```python
import math

import jax
import jax.numpy as jnp
from jax import lax
from jax.sharding import PartitionSpec as P

D = 1024
HEADS = 16
HH = 16
WW = 16


epsilon = 1e-06


def from_behind(array, axis, by):
    devices = lax.axis_size(axis)
    return lax.ppermute(array, axis, [(i, (i + by) % devices) for i in range(devices)])


def head_norm(rows, head_width):
    width = rows.shape[-1]
    group = jnp.arange(width, dtype=jnp.int32) // head_width
    averaging = (group[:, None] == group[None, :]).astype(jnp.float32) / head_width
    mean_rows = jnp.dot(rows, averaging, precision=lax.Precision.HIGHEST)
    center = rows - mean_rows
    spread = jnp.dot(center * center, averaging, precision=lax.Precision.HIGHEST)
    return center * lax.rsqrt(spread + epsilon)


def shift_down(piece, axis):
    widths = [(0, 0)] * piece.ndim
    widths[axis] = (1, 0)
    padded = jnp.pad(piece, widths)
    return lax.slice_in_dim(padded, 0, piece.shape[axis], 1, axis)


def spatial_pool(frames, taps):
    count, rows_in, cols_in, width = frames.shape
    grouped = frames.reshape(count, rows_in // 4, 4, cols_in // 4, 4 * width)
    offsets = (3, 0, 1)
    plain = jnp.zeros((count, rows_in // 4, cols_in // 4, width), jnp.float32)
    col_moved = plain
    row_moved = plain
    both_moved = plain
    for second in range(3):
        row_slab = grouped[:, :, offsets[second], :, :]
        for third in range(3):
            start = offsets[third] * width
            piece = row_slab[:, :, :, start : start + width] * taps[3 * second + third]
            if second == 0 and third == 0:
                both_moved = piece
            elif second == 0:
                row_moved = row_moved + piece
            elif third == 0:
                col_moved = col_moved + piece
            else:
                plain = plain + piece
    result = plain + shift_down(col_moved, 2)
    return result + shift_down(row_moved + shift_down(both_moved, 2), 1)


def pool_field(field, last_frame, kernel):
    count, rows_in, cols_in, width = field.shape
    paired = field.reshape(count // 2, 2, rows_in, cols_in, width)
    even_frames = paired[:, 0]
    odd_frames = paired[:, 1]
    result = spatial_pool(even_frames, kernel[9:18]) + spatial_pool(odd_frames, kernel[18:27])
    earlier_first = spatial_pool(last_frame[None], kernel[0:9])
    earlier_rest = spatial_pool(odd_frames[:-1], kernel[0:9])
    earlier_all = jnp.concatenate([earlier_first, earlier_rest], axis=0)
    return result + earlier_all


def per_device(tokens, w_query, w_key, w_value, w_out, pool_kernel):
    row_count, col_count = tokens.shape
    local_width = w_query.shape[1]
    head_width = D // HEADS
    heads_here = local_width // head_width
    frame_count = row_count // (HH * WW)
    stacked_weights = jnp.concatenate([w_query, w_key, w_value], axis=1)
    projected = jnp.dot(
        lax.all_gather(tokens, "chan", axis=1, tiled=True),
        stacked_weights,
        preferred_element_type=jnp.float32,
    ).astype(jnp.bfloat16)
    queries = projected[:, :local_width]
    key_value = projected[:, local_width:].reshape(frame_count, HH, WW, 2 * local_width)
    last_frame = from_behind(key_value[frame_count - 1], "tm", 1)
    kernel = jnp.concatenate(
        [jnp.tile(pool_kernel[0], (1, heads_here)), jnp.tile(pool_kernel[1], (1, heads_here))],
        axis=1,
    )
    pooled_rows = pool_field(key_value.astype(jnp.float32), last_frame.astype(jnp.float32), kernel)
    pooled_rows = pooled_rows.reshape(-1, 2 * local_width)
    pooled_block = head_norm(pooled_rows, head_width).astype(jnp.bfloat16)
    reach = min(6, (lax.axis_size("tm") - 1) // 2)
    collected = [pooled_block]
    onward = pooled_block
    backward_block = pooled_block
    for hop_index in range(reach):
        onward = from_behind(onward, "tm", -1)
        backward_block = from_behind(backward_block, "tm", 1)
        collected.append(onward)
        collected.append(backward_block)
    key_rows = jnp.concatenate(collected, axis=0)
    key_count = key_rows.shape[0]
    channel_head = jnp.arange(local_width, dtype=jnp.int32) // head_width
    head_mask = (jnp.arange(heads_here, dtype=jnp.int32)[:, None] == channel_head[None, :]).astype(
        jnp.bfloat16
    )
    key_spread = (key_rows[None, :, :local_width] * head_mask[:, None, :]).reshape(
        heads_here * key_count, local_width
    )
    value_spread = (key_rows[None, :, local_width:] * head_mask[:, None, :]).reshape(
        heads_here * key_count, local_width
    )
    tile_rows = min(512, row_count)
    query_tiles = queries.reshape(row_count // tile_rows, tile_rows, local_width)
    scale = 1.0 / math.sqrt(head_width)

    def attend(query_tile):
        scores = (
            lax.dot_general(
                query_tile, key_spread, (((1,), (1,)), ((), ())), preferred_element_type=jnp.float32
            )
            * scale
        )
        split = scores.reshape(tile_rows, heads_here, key_count)
        highest = jnp.max(split, axis=-1, keepdims=True)
        weighted = jnp.exp(split - highest)
        summed = jnp.sum(weighted, axis=-1)
        weights_bf = weighted.astype(jnp.bfloat16).reshape(tile_rows, heads_here * key_count)
        blended = jnp.dot(weights_bf, value_spread, preferred_element_type=jnp.float32)
        divisor = jnp.repeat(summed, head_width, axis=1)
        outcome = blended / divisor + query_tile.astype(jnp.float32)
        return outcome.astype(jnp.bfloat16)

    attended = lax.map(attend, query_tiles).reshape(row_count, local_width)
    partial_sum = jnp.dot(attended, w_out, preferred_element_type=jnp.float32)
    column_share = lax.psum_scatter(partial_sum, "chan", scatter_dimension=1, tiled=True)
    return (tokens.astype(jnp.float32) + column_share).astype(jnp.bfloat16)


def solution(mesh):
    return jax.shard_map(
        per_device,
        mesh=mesh,
        in_specs=(
            P("tm", "chan"),
            P(None, "chan"),
            P(None, "chan"),
            P(None, "chan"),
            P("chan", None),
            P(),
        ),
        out_specs=P("tm", "chan"),
        check_vma=False,
    )
```

profile of v0, /device:TPU:3, one launch (start us, length us, event | category | flops | bytes accessed | tf_op | source)
XLA Modules:
  0.0 304.7 jit_solution(4982146003979510244)
XLA Ops:
  10.8 33.6 %all-gather.2.cloned.1.call-done = bf16[2048,1024]{1,0:T(8,128)(2,1)} async-done(((bf16[2048,256]{1,0:T(8,128)(2,1)}), bf16[2048,1024]{1,0:T(8,128)(2,1)}) %all-gather.2.cloned.1.call-update) | async-done | bytes 4194320 | tf_op jit(solution)/shard_map/all_gather | solution.py:84
  44.4 6.1 %fusion.13 = bf16[2048,768]{0,1:T(8,128)(2,1)S(1)} fusion(bf16[2048,1024]{1,0:T(8,128)(2,1)} %all-gather.2.cloned.1.call-done, bf16[1024,256]{1,0:T(8,128)(2,1)} %param.11, bf16[1024,256]{1,0:T(8,128)(2,1)} %param.10, bf16[1024,256]{1,0:T(8,128)(2,1)} %param.9), kind=kOutput, calls=%fused_computation.17 | convolution fusion | flops 3227516928 | bytes 8912896 | tf_op jit(solution)/shard_map/dot_general | solution.py:83
  54.8 5.4 %copy.11 = f32[2048,512]{1,0:T(8,128)} copy(f32[2048,512]{0,1:T(8,128)} %slice_convert_fusion) | data formatting | bytes 8388608 | tf_op jit(solution)/shard_map/convert_element_type | solution.py:95
  63.0 4.3 %fusion.92 = (f32[4,1,16,16,512]{4,3,2,1,0:T(8,128)S(1)}, f32[4,1,16,16,512]{4,3,2,1,0:T(8,128)}) fusion(f32[4,2,16,16,512]{4,3,2,1,0:T(8,128)} %bitcast.135), kind=kLoop, calls=%fused_computation.168 | loop fusion | bytes 8388608 | tf_op jit(solution)/shard_map/slice | solution.py:68
  69.5 3.1 %reshape.160 = f32[3,4,4,4,2048]{4,3,2,1,0:T(4,128)} reshape(f32[3,1,16,16,512]{4,3,2,1,0:T(8,128)} %slice.500) | data formatting | bytes 3145728 | tf_op jit(solution)/shard_map/reshape | solution.py:41
  74.8 3.6 %reshape_squeeze.6 = f32[4,4,4,4,2048]{4,3,2,1,0:T(4,128)} reshape(f32[4,1,16,16,512]{4,3,2,1,0:T(8,128)} %get-tuple-element.98) | data formatting | bytes 4194304 | tf_op jit(solution)/shard_map/reshape;squeeze | solution.py:41
  95.9 4.6 %collective-permute-start.3 = (bf16[64,512]{1,0:T(8,128)(2,1)S(1)}, bf16[64,512]{1,0:T(8,128)(2,1)S(1)}, u32[]{:S(2)}, u32[]{:S(2)}) collective-permute-start(bf16[64,512]{1,0:T(8,128)(2,1)S(1)} %collective-permute-done.1), channel_id=1, source_target_pairs={{0,28},{4,0},{8,4},{12,8},{16,12},{20,16},{24,20},{28,24},{1,29},{... | collective-permute-start | bytes 196616 | tf_op jit(solution)/shard_map/ppermute | solution.py:19
  101.8 4.6 %collective-permute-start.5 = (bf16[64,512]{1,0:T(8,128)(2,1)S(1)}, bf16[64,512]{1,0:T(8,128)(2,1)S(1)}, u32[]{:S(2)}, u32[]{:S(2)}) collective-permute-start(bf16[64,512]{1,0:T(8,128)(2,1)S(1)} %collective-permute-done.3), channel_id=1, source_target_pairs={{0,28},{4,0},{8,4},{12,8},{16,12},{20,16},{24,20},{28,24},{1,29},{... | collective-permute-start | bytes 196616 | tf_op jit(solution)/shard_map/ppermute | solution.py:19
  107.7 5.6 %collective-permute-done.6 = bf16[64,512]{1,0:T(8,128)(2,1)S(1)} collective-permute-done((bf16[64,512]{1,0:T(8,128)(2,1)S(1)}, bf16[64,512]{1,0:T(8,128)(2,1)S(1)}, u32[]{:S(2)}, u32[]{:S(2)}) %collective-permute-start.6) | collective-permute-done | bytes 65568 | tf_op jit(solution)/shard_map/ppermute | solution.py:19
  114.1 104.1 %while.12 = (s32[]{:T(128)}, bf16[4,512,256]{2,1,0:T(8,128)(2,1)}, bf16[4,512,256]{2,1,0:T(8,128)(2,1)S(1)}, bf16[4,256]{1,0:T(4,128)(2,1)S(1)}, bf16[448,256]{1...) while((s32[]{:T(128)}, bf16[4,512,256]{2,1,0:T(8,128)(2,1)}, ...), condition=%wide.region_3.4_spmd.clone.clone, body=%wide.region_0.3_spmd.clone.clone.sunk | while | flops 946466816 | bytes 43756124 | solution.py:140
  117.8 5.1 %copy.46 = f32[512,1792]{0,1:T(8,128)} copy(f32[512,1792]{1,0:T(8,128)} %convolution_multiply_fusion.2) | data formatting | bytes 7340032 | tf_op jit(solution)/shard_map/while/body/eval_jaxpr/mul | solution.py:125
  130.4 5.2 %copy.48 = f32[512,1792]{1,0:T(8,128)} copy(f32[512,1792]{0,1:T(8,128)} %bitcast.130) | data formatting | bytes 7340032 | tf_op jit(solution)/shard_map/while/body/eval_jaxpr/sub | solution.py:132
  135.6 4.5 %fusion.111 = bf16[4,512,256]{2,1,0:T(8,128)(2,1)} fusion(bf16[4,512,256]{2,1,0:T(8,128)(2,1)} %get-tuple-element.199, s32[]{:T(128)} %get-tuple-element.198, f32[512,256]{1,0:T(8,128)S(1)} %copy.47, bf16[1792,256]{1,0:T(8,128)(2,1)S(1)} %bitcast.131, f32[512,1792]{1,0:T(8,128)} %convolution_multiply_fusion.2, f32[512,1792]{1,0:T(8,128)} %copy.48, ...), kind=kOutput, calls=%fused_computation.10.clone.1 | convolution fusion | flops 472121344 | bytes 9306624 | tf_op jit(solution)/shard_map/while/body/eval_jaxpr/dot_general | solution.py:135
  143.8 5.1 %copy.46 = f32[512,1792]{0,1:T(8,128)} copy(f32[512,1792]{1,0:T(8,128)} %convolution_multiply_fusion.2) | data formatting | bytes 7340032 | tf_op jit(solution)/shard_map/while/body/eval_jaxpr/mul | solution.py:125
  156.4 5.2 %copy.48 = f32[512,1792]{1,0:T(8,128)} copy(f32[512,1792]{0,1:T(8,128)} %bitcast.130) | data formatting | bytes 7340032 | tf_op jit(solution)/shard_map/while/body/eval_jaxpr/sub | solution.py:132
  161.6 4.5 %fusion.111 = bf16[4,512,256]{2,1,0:T(8,128)(2,1)} fusion(bf16[4,512,256]{2,1,0:T(8,128)(2,1)} %get-tuple-element.199, s32[]{:T(128)} %get-tuple-element.198, f32[512,256]{1,0:T(8,128)S(1)} %copy.47, bf16[1792,256]{1,0:T(8,128)(2,1)S(1)} %bitcast.131, f32[512,1792]{1,0:T(8,128)} %convolution_multiply_fusion.2, f32[512,1792]{1,0:T(8,128)} %copy.48, ...), kind=kOutput, calls=%fused_computation.10.clone.1 | convolution fusion | flops 472121344 | bytes 9306624 | tf_op jit(solution)/shard_map/while/body/eval_jaxpr/dot_general | solution.py:135
  169.8 5.1 %copy.46 = f32[512,1792]{0,1:T(8,128)} copy(f32[512,1792]{1,0:T(8,128)} %convolution_multiply_fusion.2) | data formatting | bytes 7340032 | tf_op jit(solution)/shard_map/while/body/eval_jaxpr/mul | solution.py:125
  182.5 5.2 %copy.48 = f32[512,1792]{1,0:T(8,128)} copy(f32[512,1792]{0,1:T(8,128)} %bitcast.130) | data formatting | bytes 7340032 | tf_op jit(solution)/shard_map/while/body/eval_jaxpr/sub | solution.py:132
  187.7 4.5 %fusion.111 = bf16[4,512,256]{2,1,0:T(8,128)(2,1)} fusion(bf16[4,512,256]{2,1,0:T(8,128)(2,1)} %get-tuple-element.199, s32[]{:T(128)} %get-tuple-element.198, f32[512,256]{1,0:T(8,128)S(1)} %copy.47, bf16[1792,256]{1,0:T(8,128)(2,1)S(1)} %bitcast.131, f32[512,1792]{1,0:T(8,128)} %convolution_multiply_fusion.2, f32[512,1792]{1,0:T(8,128)} %copy.48, ...), kind=kOutput, calls=%fused_computation.10.clone.1 | convolution fusion | flops 472121344 | bytes 9306624 | tf_op jit(solution)/shard_map/while/body/eval_jaxpr/dot_general | solution.py:135
  195.9 5.1 %copy.46 = f32[512,1792]{0,1:T(8,128)} copy(f32[512,1792]{1,0:T(8,128)} %convolution_multiply_fusion.2) | data formatting | bytes 7340032 | tf_op jit(solution)/shard_map/while/body/eval_jaxpr/mul | solution.py:125
  208.5 5.2 %copy.48 = f32[512,1792]{1,0:T(8,128)} copy(f32[512,1792]{0,1:T(8,128)} %bitcast.130) | data formatting | bytes 7340032 | tf_op jit(solution)/shard_map/while/body/eval_jaxpr/sub | solution.py:132
  213.7 4.5 %fusion.111 = bf16[4,512,256]{2,1,0:T(8,128)(2,1)} fusion(bf16[4,512,256]{2,1,0:T(8,128)(2,1)} %get-tuple-element.199, s32[]{:T(128)} %get-tuple-element.198, f32[512,256]{1,0:T(8,128)S(1)} %copy.47, bf16[1792,256]{1,0:T(8,128)(2,1)S(1)} %bitcast.131, f32[512,1792]{1,0:T(8,128)} %convolution_multiply_fusion.2, f32[512,1792]{1,0:T(8,128)} %copy.48, ...), kind=kOutput, calls=%fused_computation.10.clone.1 | convolution fusion | flops 472121344 | bytes 9306624 | tf_op jit(solution)/shard_map/while/body/eval_jaxpr/dot_general | solution.py:135
  218.2 5.8 %fusion.97 = f32[2048,1024]{1,0:T(8,128)} fusion(bf16[2048,256]{1,0:T(8,128)(2,1)} %bitcast.137, bf16[256,1024]{1,0:T(8,128)(2,1)S(1)} %copy-done), kind=kOutput, calls=%fused_computation.173 | convolution fusion | flops 1073741824 | bytes 9961472 | tf_op jit(solution)/shard_map/dot_general | solution.py:141
  224.0 71.0 %reduce-scatter.2.cloned.1.call-done = f32[2048,256]{1,0:T(8,128)} async-done(((f32[2048,1024]{1,0:T(8,128)}), f32[2048,256]{1,0:T(8,128)}) %reduce-scatter.2.cloned.1.call-update) | async-done | bytes 2097168 | tf_op jit(solution)/shard_map/reduce_scatter | solution.py:142
  (139 shorter events, 83.8 us)
Async XLA Ops:
  6.5 211.7 %copy-start = (bf16[256,1024]{1,0:T(8,128)(2,1)S(1)}, bf16[256,1024]{1,0:T(8,128)(2,1)}, u32[]{:S(2)}) copy-start(bf16[256,1024]{1,0:T(8,128)(2,1)} %param.12) | copy-start | bytes 1572868
  6.5 37.9 %all-gather.2.cloned.1.call-start = ((), (), s32[]{:S(2)}) async-start(), calls=%async_computation.1 | async-start | bytes 5242880 | tf_op jit(solution)/shard_map/all_gather | solution.py:84
  7.3 287.8 %reduce-scatter.2.cloned.1.call-start = ((), (), s32[]{:S(2)}) async-start(), calls=%async_computation.2 | async-start | bytes 10485760 | tf_op jit(solution)/shard_map/reduce_scatter | solution.py:142
  10.8 69.9 %copy-start.6 = (f32[1,512]{1,0:T(1,128)}, f32[1,512]{1,0:T(1,128)S(1)}, u32[]{:S(2)}) copy-start(f32[1,512]{1,0:T(1,128)S(1)} %get-tuple-element.114) | copy-start | bytes 6148
  68.1 17.5 %collective-permute-start = (bf16[16,16,512]{2,1,0:T(8,128)(2,1)}, bf16[16,16,512]{2,1,0:T(8,128)(2,1)}, u32[]{:S(2)}, u32[]{:S(2)}) collective-permute-start(bf16[16,16,512]{2,1,0:T(8,128)(2,1)} %bitcast.29), channel_id=1, source_target_pairs={{0,4},{4,8},{8,12},{12,16},{16,20},{20,24},{24,28},{28,0},{1,5},{5... | collective-permute-start | bytes 786440 | tf_op jit(solution)/shard_map/ppermute | solution.py:19
  80.7 3.2 %copy-start.4 = (f32[3,4,4,2048]{3,2,1,0:T(4,128)S(1)}, f32[3,4,4,2048]{3,2,1,0:T(4,128)}, u32[]{:S(2)}) copy-start(f32[3,4,4,2048]{3,2,1,0:T(4,128)} %get-tuple-element.105) | copy-start | bytes 1179652
  80.7 3.2 %copy-start.5 = (f32[3,4,4,2048]{3,2,1,0:T(4,128)S(1)}, f32[3,4,4,2048]{3,2,1,0:T(4,128)}, u32[]{:S(2)}) copy-start(f32[3,4,4,2048]{3,2,1,0:T(4,128)} %get-tuple-element.106) | copy-start | bytes 1179652
  80.7 3.2 %copy-start.17 = (f32[1,512]{1,0:T(1,128)S(1)}, f32[1,512]{1,0:T(1,128)}, u32[]{:S(2)}) copy-start(f32[1,512]{1,0:T(1,128)} %get-tuple-element.126) | copy-start | bytes 6148
  80.8 3.2 %copy-start.18 = (f32[1,512]{1,0:T(1,128)S(1)}, f32[1,512]{1,0:T(1,128)}, u32[]{:S(2)}) copy-start(f32[1,512]{1,0:T(1,128)} %get-tuple-element.127) | copy-start | bytes 6148
  80.8 3.3 %copy-start.8 = (f32[1,512]{1,0:T(1,128)S(1)}, f32[1,512]{1,0:T(1,128)}, u32[]{:S(2)}) copy-start(f32[1,512]{1,0:T(1,128)} %get-tuple-element.119) | copy-start | bytes 6148
  80.8 3.3 %copy-start.9 = (f32[1,512]{1,0:T(1,128)S(1)}, f32[1,512]{1,0:T(1,128)}, u32[]{:S(2)}) copy-start(f32[1,512]{1,0:T(1,128)} %get-tuple-element.120) | copy-start | bytes 6148
  80.8 3.3 %copy-start.10 = (f32[1,512]{1,0:T(1,128)S(1)}, f32[1,512]{1,0:T(1,128)}, u32[]{:S(2)}) copy-start(f32[1,512]{1,0:T(1,128)} %get-tuple-element.121) | copy-start | bytes 6148
  80.8 3.3 %copy-start.11 = (f32[1,512]{1,0:T(1,128)S(1)}, f32[1,512]{1,0:T(1,128)}, u32[]{:S(2)}) copy-start(f32[1,512]{1,0:T(1,128)} %get-tuple-element.122) | copy-start | bytes 6148
  80.8 4.0 %copy-start.14 = (f32[1,512]{1,0:T(1,128)S(1)}, f32[1,512]{1,0:T(1,128)}, u32[]{:S(2)}) copy-start(f32[1,512]{1,0:T(1,128)} %get-tuple-element.134) | copy-start | bytes 6148
  80.8 4.0 %copy-start.15 = (f32[1,512]{1,0:T(1,128)S(1)}, f32[1,512]{1,0:T(1,128)}, u32[]{:S(2)}) copy-start(f32[1,512]{1,0:T(1,128)} %get-tuple-element.135) | copy-start | bytes 6148
  83.0 3.9 %copy-start.7 = (f32[1,512]{1,0:T(1,128)S(1)}, f32[1,512]{1,0:T(1,128)}, u32[]{:S(2)}) copy-start(f32[1,512]{1,0:T(1,128)} %copy-done.6) | copy-start | bytes 6148
  87.1 8.2 %slice-start = ((bf16[2048,768]{0,1:T(8,128)(2,1)}), bf16[2048,256]{0,1:T(8,128)(2,1)S(1)}, s32[]{:S(2)}) async-start(bf16[2048,768]{0,1:T(8,128)(2,1)} %copy-done.1), calls=%async_computation.3 | async-start | bytes 2097152 | tf_op jit(solution)/shard_map/slice | solution.py:88
  91.7 4.2 %collective-permute-start.1 = (bf16[64,512]{1,0:T(8,128)(2,1)S(1)}, bf16[64,512]{1,0:T(8,128)(2,1)S(1)}, u32[]{:S(2)}, u32[]{:S(2)}) collective-permute-start(bf16[64,512]{1,0:T(8,128)(2,1)S(1)} %get-tuple-element.143), channel_id=1, source_target_pairs={{0,28},{4,0},{8,4},{12,8},{16,12},{20,16},{24,20},{28,24},{1,29},{... | collective-permute-start | bytes 196616 | tf_op jit(solution)/shard_map/ppermute | solution.py:19
  95.8 5.9 %collective-permute-start.2 = (bf16[64,512]{1,0:T(8,128)(2,1)S(1)}, bf16[64,512]{1,0:T(8,128)(2,1)S(1)}, u32[]{:S(2)}, u32[]{:S(2)}) collective-permute-start(bf16[64,512]{1,0:T(8,128)(2,1)S(1)} %get-tuple-element.143), channel_id=1, source_target_pairs={{0,4},{4,8},{8,12},{12,16},{16,20},{20,24},{24,28},{28,0},{1,5},{5... | collective-permute-start | bytes 196616 | tf_op jit(solution)/shard_map/ppermute | solution.py:19
  95.9 5.9 %collective-permute-start.3 = (bf16[64,512]{1,0:T(8,128)(2,1)S(1)}, bf16[64,512]{1,0:T(8,128)(2,1)S(1)}, u32[]{:S(2)}, u32[]{:S(2)}) collective-permute-start(bf16[64,512]{1,0:T(8,128)(2,1)S(1)} %collective-permute-done.1), channel_id=1, source_target_pairs={{0,28},{4,0},{8,4},{12,8},{16,12},{20,16},{24,20},{28,24},{1,29},{... | collective-permute-start | bytes 196616 | tf_op jit(solution)/shard_map/ppermute | solution.py:19
  101.6 5.8 %collective-permute-start.4 = (bf16[64,512]{1,0:T(8,128)(2,1)S(1)}, bf16[64,512]{1,0:T(8,128)(2,1)S(1)}, u32[]{:S(2)}, u32[]{:S(2)}) collective-permute-start(bf16[64,512]{1,0:T(8,128)(2,1)S(1)} %collective-permute-done.2), channel_id=1, source_target_pairs={{0,4},{4,8},{8,12},{12,16},{16,20},{20,24},{24,28},{28,0},{1,5},{5... | collective-permute-start | bytes 196616 | tf_op jit(solution)/shard_map/ppermute | solution.py:19
  101.8 5.9 %collective-permute-start.5 = (bf16[64,512]{1,0:T(8,128)(2,1)S(1)}, bf16[64,512]{1,0:T(8,128)(2,1)S(1)}, u32[]{:S(2)}, u32[]{:S(2)}) collective-permute-start(bf16[64,512]{1,0:T(8,128)(2,1)S(1)} %collective-permute-done.3), channel_id=1, source_target_pairs={{0,28},{4,0},{8,4},{12,8},{16,12},{20,16},{24,20},{28,24},{1,29},{... | collective-permute-start | bytes 196616 | tf_op jit(solution)/shard_map/ppermute | solution.py:19
  107.5 5.8 %collective-permute-start.6 = (bf16[64,512]{1,0:T(8,128)(2,1)S(1)}, bf16[64,512]{1,0:T(8,128)(2,1)S(1)}, u32[]{:S(2)}, u32[]{:S(2)}) collective-permute-start(bf16[64,512]{1,0:T(8,128)(2,1)S(1)} %collective-permute-done.4), channel_id=1, source_target_pairs={{0,4},{4,8},{8,12},{12,16},{16,20},{20,24},{24,28},{28,0},{1,5},{5... | collective-permute-start | bytes 196616 | tf_op jit(solution)/shard_map/ppermute | solution.py:19
  224.0 71.1 %copy-start.2 = (bf16[2048,256]{1,0:T(8,128)(2,1)S(1)}, bf16[2048,256]{1,0:T(8,128)(2,1)}, u32[]{:S(2)}) copy-start(bf16[2048,256]{1,0:T(8,128)(2,1)} %param.8) | copy-start | bytes 3145732
  (8 other events, 19.0 us)
Sparse Core Ops, SparseCore 0:
  8.9 35.5 all-gather.1
  224.1 70.8 reduce-scatter.1
where the time goes:
time: 309 us; the launch traced here: 305 us
  waiting for transfers between devices  114 us (37%)
  local copies, waits for them, and re-layouts  85.1 us (28%)
  matrix products  43 us (14%)
  other arithmetic  35.5 us (11%)
  between operations  13.9 us (4%)
  starting transfers between devices  13.5 us (4%)
    reduce_scatter x1, waiting for transfers between devices, per_device(): lax.psum_scatter(partial_sum, 'chan', scatter_dimension=1, tiled=True)  71 us
    all_gather x1, waiting for transfers between devices, per_device(): lax.all_gather(tokens, 'chan', axis=1, tiled=True)  33.6 us
    sub x8, local copies, waits for them, and re-layouts, attend(): weighted = jnp.exp(split - highest)  30.3 us
    mul x4, local copies, waits for them, and re-layouts, attend(): lax.dot_general(query_tile, key_spread, (((1,), (1,)), ((), ())), preferr...  20.5 us
    dot_general x4, matrix products, attend(): jnp.dot(weights_bf, value_spread, preferred_element_type=jnp.float32)  18.1 us
    ppermute x7, starting transfers between devices, from_behind(): lax.ppermute(array, axis, [(i, (i + by) % devices) for i in range(devices)])  13.4 us
    reduce_sum x4, other arithmetic, attend(): summed = jnp.sum(weighted, axis=-1)  10.2 us
    dot_general x4, matrix products, attend(): lax.dot_general(query_tile, key_spread, (((1,), (1,)), ((), ())), preferr...  9.88 us
  transfers between devices with their start and end apart: 9, of which 8 were waited for; matrix products, arithmetic and copies ran while one was open for 7% of the time, Pallas kernels for 0%

commit v1 on v0

v1 whole, which is shorter than its diff:
```python
import functools

import jax
import jax.numpy as jnp
from jax import lax
from jax.experimental import pallas as pl
from jax.experimental.pallas import tpu as pltpu
from jax.sharding import PartitionSpec as P

D = 1024
HEADS = 16
HDIM = 64
HH = 16
WW = 16
FRAME = HH * WW
EPSILON = 1e-06
MESH = pl.DeviceIdType.MESH
HIGHEST = lax.Precision.HIGHEST
f32 = jnp.float32
bf16 = jnp.bfloat16


def kernel(
    n_tm, reach, frames, width,
    tokens, w_query, w_key, w_value, w_out, pool_kernel, out,
    tok, weights, wo, queries, field, taps, pre, halo_out, halo_in, gathered, k_big, v_big, att,
    local_sem, tok_send, tok_recv, wo_send, wo_recv, halo_send, halo_recv,
    gat_send, gat_recv, att_send, att_recv,
):
    tm = lax.axis_index("tm")
    me = lax.axis_index("chan")
    sib = me + 1 - 2 * lax.rem(me, 2)
    across = lax.rem(me + 2, 4)
    diag = lax.rem(sib + 2, 4)
    heads = width // HDIM
    pairs = frames // 2
    offsets = [d for d in range(-reach, reach + 1) if d != 0]

    def tm_at(d):
        return lax.rem(tm + d + n_tm, n_tm)

    def rows_of(frame):
        return pl.ds(pl.multiple_of(frame * FRAME, FRAME), FRAME)

    loads = [
        pltpu.make_async_copy(w_query, weights.at[:, pl.ds(0, width)], local_sem.at[0]),
        pltpu.make_async_copy(w_key, weights.at[:, pl.ds(width, width)], local_sem.at[1]),
        pltpu.make_async_copy(w_value, weights.at[:, pl.ds(2 * width, width)], local_sem.at[2]),
        pltpu.make_async_copy(tokens, tok.at[me], local_sem.at[3]),
        pltpu.make_async_copy(
            w_out.at[:, pl.ds(pl.multiple_of(me * width, width), width)], wo.at[me], local_sem.at[4]
        ),
    ]
    for load in loads:
        load.start()

    barrier = pltpu.get_barrier_semaphore()
    for other in (sib, across, diag):
        pl.semaphore_signal(barrier, inc=1, device_id={"chan": other}, device_id_type=MESH)
    for d in offsets:
        pl.semaphore_signal(barrier, inc=1, device_id={"tm": tm_at(d)}, device_id_type=MESH)
    pl.semaphore_wait(barrier, 3 + len(offsets))

    def token_copy(kind, frame):
        rows = rows_of(frame)
        if kind == 2:
            source, slot = tok.at[across, rows], across
        else:
            source, slot = tokens.at[rows], me
        return pltpu.make_async_remote_copy(
            src_ref=source, dst_ref=tok.at[slot, rows],
            send_sem=tok_send.at[kind, frame], recv_sem=tok_recv.at[kind, frame],
            device_id={"chan": across if kind == 0 else sib}, device_id_type=MESH,
        )

    def token_arrival(kind, frame):
        rows = rows_of(frame)
        slot = (across, sib, diag)[kind]
        return pltpu.make_async_remote_copy(
            src_ref=tok.at[slot, rows], dst_ref=tok.at[slot, rows],
            send_sem=tok_send.at[kind, frame], recv_sem=tok_recv.at[kind, frame],
            device_id={"chan": across if kind == 0 else sib}, device_id_type=MESH,
        )

    def att_copy(kind, frame):
        rows = rows_of(frame)
        slot = across if kind == 2 else me
        return pltpu.make_async_remote_copy(
            src_ref=att.at[slot, rows], dst_ref=att.at[slot, rows],
            send_sem=att_send.at[kind, frame], recv_sem=att_recv.at[kind, frame],
            device_id={"chan": across if kind == 0 else sib}, device_id_type=MESH,
        )

    def att_arrival(kind, frame):
        rows = rows_of(frame)
        slot = (across, sib, diag)[kind]
        return pltpu.make_async_remote_copy(
            src_ref=att.at[slot, rows], dst_ref=att.at[slot, rows],
            send_sem=att_send.at[kind, frame], recv_sem=att_recv.at[kind, frame],
            device_id={"chan": across if kind == 0 else sib}, device_id_type=MESH,
        )

    def pair_at(step):
        return lax.rem(step + pairs - 1, pairs)

    @pl.loop(0, pairs)
    def _(step):
        for second in range(2):
            frame = 2 * pair_at(step) + second
            token_copy(0, frame).start()
            token_copy(1, frame).start()

    wo_copies = []
    for index, other in enumerate((sib, across, diag)):
        copy = pltpu.make_async_remote_copy(
            src_ref=w_out.at[:, pl.ds(pl.multiple_of(other * width, width), width)],
            dst_ref=wo.at[me], send_sem=wo_send.at[index], recv_sem=wo_recv.at[index],
            device_id={"chan": other}, device_id_type=MESH,
        )
        copy.start()
        wo_copies.append(copy)

    channel = lax.broadcasted_iota(jnp.int32, (HDIM, 2 * width), 1)
    inner = lax.broadcasted_iota(jnp.int32, (HDIM, 2 * width), 0)
    same = lax.rem(channel, HDIM) == inner
    spread_k = (same & (channel < width)).astype(f32)
    spread_v = (same & (channel >= width)).astype(f32)
    wide = jnp.dot(pool_kernel[0], spread_k, precision=HIGHEST, preferred_element_type=f32)
    wide = wide + jnp.dot(pool_kernel[1], spread_v, precision=HIGHEST, preferred_element_type=f32)
    column = lax.broadcasted_iota(jnp.int32, (WW, 2 * width), 0)
    place = lax.rem(column, 4)
    for tap in range(9):
        line = jnp.where((place == 3) & (column < WW - 1), wide[3 * tap : 3 * tap + 1], 0.0)
        line = jnp.where(place == 0, wide[3 * tap + 1 : 3 * tap + 2], line)
        line = jnp.where(place == 1, wide[3 * tap + 2 : 3 * tap + 3], line)
        taps[tap] = line
    pre[...] = jnp.zeros_like(pre)

    def slab(slot, first, i):
        total = None
        for second in range(3):
            row = 4 * i - 1 + second
            if row < 0:
                continue
            term = field[slot, row] * taps[3 * first + second]
            total = term if total is None else total + term
        return total

    def column_sum(block):
        rows_in = block.shape[0]
        r = lax.broadcasted_iota(jnp.int32, (rows_in // 4, rows_in), 0)
        c = lax.broadcasted_iota(jnp.int32, (rows_in // 4, rows_in), 1)
        pick = ((c >= 4 * r - 1) & (c <= 4 * r + 1)).astype(f32)
        return jnp.dot(pick, block, precision=HIGHEST, preferred_element_type=f32)

    halo = pltpu.make_async_remote_copy(
        src_ref=halo_out, dst_ref=halo_in, send_sem=halo_send, recv_sem=halo_recv,
        device_id={"tm": tm_at(1)}, device_id_type=MESH,
    )

    for load in loads[:4]:
        load.wait()

    @pl.loop(0, pairs)
    def _(step):
        pair = pair_at(step)
        for second in range(2):
            frame = 2 * pair + second
            token_arrival(0, frame).wait_recv()
            token_copy(2, frame).start()
        for second in range(2):
            frame = 2 * pair + second
            rows = rows_of(frame)
            token_arrival(1, frame).wait_recv()
            token_arrival(2, frame).wait_recv()
            total = None
            for s in range(4):
                term = jnp.dot(
                    tok[s, rows], weights[s * width : (s + 1) * width, :], preferred_element_type=f32
                )
                total = term if total is None else total + term
            total = total.astype(bf16)
            queries[rows, :] = total[:, :width]
            field[second] = total[:, width:].astype(f32).reshape(HH, WW, 2 * width)
        for i in range(HH // 4):
            pre[pair, i] = pre[pair, i] + slab(0, 1, i) + slab(1, 2, i)
            pre[pair + 1, i] = pre[pair + 1, i] + slab(1, 0, i)

        @pl.when(step == 0)
        def _():
            halo_out[...] = column_sum(pre[pairs].reshape(HH // 4 * WW, 2 * width))
            halo.start()

    pooled = column_sum(pre[0:pairs].reshape(pairs * HH // 4 * WW, 2 * width))
    halo.wait_recv()
    block_rows = pooled.shape[0]
    halo_rows = HH // 4 * (WW // 4)
    pooled = jnp.concatenate([pooled[:halo_rows] + halo_in[...], pooled[halo_rows:]], axis=0)
    g0 = lax.broadcasted_iota(jnp.int32, (width, width), 0) // HDIM
    g1 = lax.broadcasted_iota(jnp.int32, (width, width), 1) // HDIM
    averaging = jnp.where(g0 == g1, 1.0 / HDIM, 0.0).astype(f32)
    for part in range(2):
        x = pooled[:, part * width : (part + 1) * width]
        center = x - jnp.dot(x, averaging, precision=HIGHEST, preferred_element_type=f32)
        spread = jnp.dot(center * center, averaging, precision=HIGHEST, preferred_element_type=f32)
        gathered[reach, :, part * width : (part + 1) * width] = (
            center * lax.rsqrt(spread + EPSILON)
        ).astype(bf16)

    sends = []
    for index, d in enumerate(offsets):
        copy = pltpu.make_async_remote_copy(
            src_ref=gathered.at[reach], dst_ref=gathered.at[reach - d],
            send_sem=gat_send.at[index], recv_sem=gat_recv.at[reach - d],
            device_id={"tm": tm_at(d)}, device_id_type=MESH,
        )
        copy.start()
        sends.append(copy)

    lane_head = lax.broadcasted_iota(jnp.int32, (block_rows, width), 1) // HDIM

    def spread_block(slot):
        rows = slice(slot * block_rows, (slot + 1) * block_rows)
        keys = gathered[slot, :, :width]
        values = gathered[slot, :, width:]
        for h in range(heads):
            k_big[h, rows, :] = keys * jnp.where(lane_head == h, HDIM**-0.5, 0.0).astype(bf16)
            v_big[h, rows, :] = values * jnp.where(lane_head == h, 1.0, 0.0).astype(bf16)

    spread_block(reach)
    for index, d in enumerate(offsets):
        slot = reach + d
        pltpu.make_async_remote_copy(
            src_ref=gathered.at[reach], dst_ref=gathered.at[slot],
            send_sem=gat_send.at[index], recv_sem=gat_recv.at[slot],
            device_id={"tm": tm_at(d)}, device_id_type=MESH,
        ).wait_recv()
        spread_block(slot)

    out_head = lax.broadcasted_iota(jnp.int32, (FRAME, width), 1) // HDIM

    @pl.loop(0, frames)
    def _(frame):
        rows = rows_of(frame)
        q = queries[rows, :]
        blended = None
        divisor = None
        for h in range(heads):
            scores = lax.dot_general(
                q, k_big[h], (((1,), (1,)), ((), ())), preferred_element_type=f32
            )
            weighted = jnp.exp(scores - jnp.max(scores, axis=-1, keepdims=True))
            summed = jnp.sum(weighted, axis=-1, keepdims=True)
            term = jnp.dot(weighted.astype(bf16), v_big[h], preferred_element_type=f32)
            blended = term if blended is None else blended + term
            wide_sum = jnp.broadcast_to(summed, (FRAME, width))
            divisor = wide_sum if divisor is None else jnp.where(out_head == h, wide_sum, divisor)
        att[me, rows] = (blended / divisor + q.astype(f32)).astype(bf16)
        att_copy(0, frame).start()
        att_copy(1, frame).start()

    loads[4].wait()
    for index, other in enumerate((sib, across, diag)):
        pltpu.make_async_remote_copy(
            src_ref=wo.at[other], dst_ref=wo.at[other],
            send_sem=wo_send.at[index], recv_sem=wo_recv.at[index],
            device_id={"chan": other}, device_id_type=MESH,
        ).wait_recv()

    @pl.loop(0, frames)
    def _(frame):
        rows = rows_of(frame)
        att_arrival(0, frame).wait_recv()
        att_copy(2, frame).start()
        att_arrival(1, frame).wait_recv()
        att_arrival(2, frame).wait_recv()
        total = tok[me, rows].astype(f32)
        for s in range(4):
            total = total + jnp.dot(att[s, rows], wo[s], preferred_element_type=f32)
        out[rows, :] = total.astype(bf16)

    @pl.loop(0, frames)
    def _(frame):
        for kind in range(3):
            token_copy(kind, frame).wait_send()
            att_copy(kind, frame).wait_send()

    for copy in wo_copies + sends + [halo]:
        copy.wait_send()


def per_device(n_tm, n_chan, tokens, w_query, w_key, w_value, w_out, pool_kernel):
    rows, width = tokens.shape
    frames = rows // FRAME
    pairs = frames // 2
    block = pairs * (HH // 4) * (WW // 4)
    reach = min(6, (n_tm - 1) // 2)
    spans = 2 * reach + 1
    heads = width // HDIM
    dma = pltpu.SemaphoreType.DMA
    anywhere = pl.BlockSpec(memory_space=pl.ANY)
    vmem = pl.BlockSpec(memory_space=pltpu.VMEM)
    return pl.pallas_call(
        functools.partial(kernel, n_tm, reach, frames, width),
        out_shape=jax.ShapeDtypeStruct((rows, width), bf16),
        in_specs=[anywhere] * 5 + [vmem],
        out_specs=vmem,
        scratch_shapes=[
            pltpu.VMEM((n_chan, rows, width), bf16),
            pltpu.VMEM((D, 3 * width), bf16),
            pltpu.VMEM((n_chan, width, width), bf16),
            pltpu.VMEM((rows, width), bf16),
            pltpu.VMEM((2, HH, WW, 2 * width), f32),
            pltpu.VMEM((9, WW, 2 * width), f32),
            pltpu.VMEM((pairs + 1, HH // 4, WW, 2 * width), f32),
            pltpu.VMEM((HH // 4 * (WW // 4), 2 * width), f32),
            pltpu.VMEM((HH // 4 * (WW // 4), 2 * width), f32),
            pltpu.VMEM((spans, block, 2 * width), bf16),
            pltpu.VMEM((heads, spans * block, width), bf16),
            pltpu.VMEM((heads, spans * block, width), bf16),
            pltpu.VMEM((n_chan, rows, width), bf16),
            dma((5,)),
            dma((3, frames)),
            dma((3, frames)),
            dma((3,)),
            dma((3,)),
            dma,
            dma,
            dma((2 * reach,)),
            dma((spans,)),
            dma((3, frames)),
            dma((3, frames)),
        ],
        compiler_params=pltpu.CompilerParams(
            collective_id=0, has_side_effects=True, vmem_limit_bytes=48 * 1024 * 1024
        ),
    )(tokens, w_query, w_key, w_value, w_out, pool_kernel)


def solution(mesh):
    shape = dict(mesh.shape)
    return jax.shard_map(
        functools.partial(per_device, shape["tm"], shape["chan"]),
        mesh=mesh,
        in_specs=(
            P("tm", "chan"),
            P(None, "chan"),
            P(None, "chan"),
            P(None, "chan"),
            P("chan", None),
            P(),
        ),
        out_specs=P("tm", "chan"),
        check_vma=False,
    )
```

time: 309 us -> 79.2 us (0.26); the launches traced: 305 us -> 78.8 us
  waiting for transfers between devices: 114 us -> 0 us
  local copies, waits for them, and re-layouts: 85.1 us -> 7.11 us
  Pallas kernels: 0 us -> 71.6 us
  matrix products: 43 us -> 0 us
  other arithmetic: 35.5 us -> 0 us
  between operations: 13.9 us -> 0.01 us
  starting transfers between devices: 13.5 us -> 0 us
    pallas_call x0 -> x1, Pallas kernels: none -> 71.6 us  [per_device(): pl.pallas_call(functools.partial(kernel, n_tm, reach, frames, width), out...]
    reduce_scatter x1 -> x0, waiting for transfers between devices: 71 us -> none  [per_device(): lax.psum_scatter(partial_sum, 'chan', scatter_dimension=1, tiled=True)]
    dot_general x12 -> x0, matrix products: 43 us -> none  [the longest x4 18.1 us: attend(): jnp.dot(weights_bf, value_spread, preferred_element_type=jnp.float32)]
    all_gather x1 -> x0, waiting for transfers between devices: 33.6 us -> none  [per_device(): lax.all_gather(tokens, 'chan', axis=1, tiled=True)]
    sub x8 -> x0, local copies, waits for them, and re-layouts: 30.3 us -> none  [attend(): weighted = jnp.exp(split - highest)]
    mul x4 -> x0, local copies, waits for them, and re-layouts: 20.5 us -> none  [attend(): lax.dot_general(query_tile, key_spread, (((1,), (1,)), ((), ())), preferr...]
    ppermute x7 -> x0, starting transfers between devices: 13.4 us -> none  [from_behind(): lax.ppermute(array, axis, [(i, (i + by) % devices) for i in range(devices)])]
    slice x10 -> x0, local copies, waits for them, and re-layouts: 10.9 us -> none  [the longest x1 4.26 us: pool_field(): odd_frames = paired[:, 1]]
  transfers between devices with their start and end apart: 9 -> 0, of which waited for: 8 -> 0; matrix products, arithmetic and copies ran while one was open for 7% -> 0% of each run, Pallas kernels for 0% -> 0%
where the time goes in v1:
time: 79.2 us; the launch traced here: 78.8 us
  Pallas kernels  71.6 us (90%)
  local copies, waits for them, and re-layouts  7.11 us (9%)
    pallas_call x1, Pallas kernels, per_device(): pl.pallas_call(functools.partial(kernel, n_tm, reach, frames, width), out...  71.6 us
    unnamed x12, local copies, waits for them, and re-layouts  7.11 us

profile of v1, /device:TPU:3, one launch (start us, length us, event | category | flops | bytes accessed | tf_op | source)
XLA Modules:
  0.0 78.8 jit_solution(15100615938250708672)
XLA Ops:
  0.0 0.7 copy.7.pool_kernel
  0.7 0.0 copy-start
  0.8 1.2 %copy-done = bf16[2048,256]{1,0:T(8,128)(2,1)S(1)} copy-done((bf16[2048,256]{1,0:T(8,128)(2,1)S(1)}, bf16[2048,256]{1,0:T(8,128)(2,1)}, u32[]{:S(2)}) %copy-start) | copy-done | bytes 1048600
  2.0 0.0 copy-start.1
  2.0 1.0 %copy-done.1 = bf16[1024,256]{1,0:T(8,128)(2,1)S(1)} copy-done((bf16[1024,256]{1,0:T(8,128)(2,1)S(1)}, bf16[1024,256]{1,0:T(8,128)(2,1)}, u32[]{:S(2)}) %copy-start.1) | copy-done | bytes 524312
  3.0 0.0 copy-start.2
  3.0 1.0 %copy-done.2 = bf16[1024,256]{1,0:T(8,128)(2,1)S(1)} copy-done((bf16[1024,256]{1,0:T(8,128)(2,1)S(1)}, bf16[1024,256]{1,0:T(8,128)(2,1)}, u32[]{:S(2)}) %copy-start.2) | copy-done | bytes 524312
  4.1 0.0 copy-start.3
  4.1 1.0 %copy-done.3 = bf16[1024,256]{1,0:T(8,128)(2,1)S(1)} copy-done((bf16[1024,256]{1,0:T(8,128)(2,1)S(1)}, bf16[1024,256]{1,0:T(8,128)(2,1)}, u32[]{:S(2)}) %copy-start.3) | copy-done | bytes 524312
  5.1 0.0 copy-start.4
  5.1 1.0 %copy-done.4 = bf16[256,1024]{1,0:T(8,128)(2,1)S(1)} copy-done((bf16[256,1024]{1,0:T(8,128)(2,1)S(1)}, bf16[256,1024]{1,0:T(8,128)(2,1)}, u32[]{:S(2)}) %copy-start.4) | copy-done | bytes 524312
  6.1 71.6 %shard_map.64 = bf16[2048,256]{1,0:T(8,128)(2,1)S(1)} custom-call(bf16[2048,256]{1,0:T(8,128)(2,1)S(1)} %copy-done, bf16[1024,256]{1,0:T(8,128)(2,1)S(1)} %copy-done.1, bf16[1024,256]{1,0:T(8,128)(2,1)S(1)} %copy-done.2, bf16[1024,256]{1,0:T(8,128)(2,1)S(1)} %copy-done.3, bf16[256,1024]{1,0:T(8,128)(2,1)S(1)} %copy-done.4, f32[2,27,64]{2,1,0:T(8,128)S(1)} %copy.7.pool_kernel), custom_call_target="tpu_custom_call" | custom-call | tf_op jit(solution)/shard_map/pallas_call | solution.py:303
  77.8 1.0 %copy.9 = bf16[2048,256]{1,0:T(8,128)(2,1)} copy(bf16[2048,256]{1,0:T(8,128)(2,1)S(1)} %shard_map.64) | data formatting | bytes 2097152
Async XLA Ops:
  0.7 1.2 %copy-start = (bf16[2048,256]{1,0:T(8,128)(2,1)S(1)}, bf16[2048,256]{1,0:T(8,128)(2,1)}, u32[]{:S(2)}) copy-start(bf16[2048,256]{1,0:T(8,128)(2,1)} %tokens.1) | copy-start | bytes 3145732
  2.0 1.0 %copy-start.1 = (bf16[1024,256]{1,0:T(8,128)(2,1)S(1)}, bf16[1024,256]{1,0:T(8,128)(2,1)}, u32[]{:S(2)}) copy-start(bf16[1024,256]{1,0:T(8,128)(2,1)} %w_query.1) | copy-start | bytes 1572868
  3.0 1.0 %copy-start.2 = (bf16[1024,256]{1,0:T(8,128)(2,1)S(1)}, bf16[1024,256]{1,0:T(8,128)(2,1)}, u32[]{:S(2)}) copy-start(bf16[1024,256]{1,0:T(8,128)(2,1)} %w_key.1) | copy-start | bytes 1572868
  4.1 1.0 %copy-start.3 = (bf16[1024,256]{1,0:T(8,128)(2,1)S(1)}, bf16[1024,256]{1,0:T(8,128)(2,1)}, u32[]{:S(2)}) copy-start(bf16[1024,256]{1,0:T(8,128)(2,1)} %w_value.1) | copy-start | bytes 1572868
  5.1 1.0 %copy-start.4 = (bf16[256,1024]{1,0:T(8,128)(2,1)S(1)}, bf16[256,1024]{1,0:T(8,128)(2,1)}, u32[]{:S(2)}) copy-start(bf16[256,1024]{1,0:T(8,128)(2,1)} %w_out.1) | copy-start | bytes 1572868

commit v2 on v1

v2 whole, which is shorter than its diff:
```python
import functools

import jax
import jax.numpy as jnp
from jax import lax
from jax.experimental import pallas as pl
from jax.experimental.pallas import tpu as pltpu
from jax.sharding import PartitionSpec as P

D = 1024
HEADS = 16
HDIM = 64
HH = 16
WW = 16
FRAME = HH * WW
EPSILON = 1e-06
MESH = pl.DeviceIdType.MESH
HIGHEST = lax.Precision.HIGHEST
f32 = jnp.float32
bf16 = jnp.bfloat16


def kernel(
    n_tm, reach, frames, width,
    tokens, w_query, w_key, w_value, w_out, pool_hbm, out,
    pool_kernel, tok, weights, wo, queries, field, taps, pre, halo_out, halo_in, gathered, k_big, v_big, att,
    local_sem, tok_send, tok_recv, wo_send, wo_recv, halo_send, halo_recv,
    gat_send, gat_recv, att_send, att_recv,
):
    tm = lax.axis_index("tm")
    me = lax.axis_index("chan")
    sib = me + 1 - 2 * lax.rem(me, 2)
    across = lax.rem(me + 2, 4)
    diag = lax.rem(sib + 2, 4)
    heads = width // HDIM
    pairs = frames // 2
    relayed = n_tm == 8
    beside = tm + 1 - 2 * lax.rem(tm, 2)
    offsets = [-2, -1, 1, 2, 4] if relayed else [d for d in range(-reach, reach + 1) if d != 0]

    def tm_at(d):
        return lax.rem(tm + d + n_tm, n_tm)

    def rows_of(frame):
        return pl.ds(pl.multiple_of(frame * FRAME, FRAME), FRAME)

    loads = [
        pltpu.make_async_copy(w_query, weights.at[:, pl.ds(0, width)], local_sem.at[0]),
        pltpu.make_async_copy(w_key, weights.at[:, pl.ds(width, width)], local_sem.at[1]),
        pltpu.make_async_copy(w_value, weights.at[:, pl.ds(2 * width, width)], local_sem.at[2]),
        pltpu.make_async_copy(tokens, tok.at[me], local_sem.at[3]),
        pltpu.make_async_copy(
            w_out.at[:, pl.ds(pl.multiple_of(me * width, width), width)], wo.at[me], local_sem.at[4]
        ),
        pltpu.make_async_copy(pool_hbm, pool_kernel, local_sem.at[5]),
    ]
    for load in loads:
        load.start()

    barrier = pltpu.get_barrier_semaphore()
    for other in (sib, across, diag):
        pl.semaphore_signal(barrier, inc=1, device_id={"chan": other}, device_id_type=MESH)
    for d in offsets:
        pl.semaphore_signal(barrier, inc=1, device_id={"tm": tm_at(d)}, device_id_type=MESH)
    pl.semaphore_wait(barrier, 3 + len(offsets))

    def part_of(ref, pair, part):
        both = pl.ds(2 * pair, 2)
        if part == 0:
            return ref.at[both, :, pl.ds(0, 2)]
        if part == 1:
            return ref.at[both, pl.ds(0, 3), 3]
        if part == 2:
            return ref.at[both, :, 2]
        return ref.at[both, 3, 3]

    def token_copy(kind, pair, part):
        if kind == 2:
            source, slot = part_of(tok.at[across], pair, part), across
        else:
            source, slot = part_of(tokens, pair, part), me
        return pltpu.make_async_remote_copy(
            src_ref=source, dst_ref=part_of(tok.at[slot], pair, part),
            send_sem=tok_send.at[kind, pair, part], recv_sem=tok_recv.at[kind, pair, part],
            device_id={"chan": across if kind == 0 else sib}, device_id_type=MESH,
        )

    def token_arrival(kind, pair, part):
        place = part_of(tok.at[(across, sib, diag)[kind]], pair, part)
        return pltpu.make_async_remote_copy(
            src_ref=place, dst_ref=place,
            send_sem=tok_send.at[kind, pair, part], recv_sem=tok_recv.at[kind, pair, part],
            device_id={"chan": across if kind == 0 else sib}, device_id_type=MESH,
        )

    def att_copy(kind, frame):
        rows = rows_of(frame)
        slot = across if kind == 2 else me
        return pltpu.make_async_remote_copy(
            src_ref=att.at[slot, rows], dst_ref=att.at[slot, rows],
            send_sem=att_send.at[kind, frame], recv_sem=att_recv.at[kind, frame],
            device_id={"chan": across if kind == 0 else sib}, device_id_type=MESH,
        )

    def att_arrival(kind, frame):
        rows = rows_of(frame)
        slot = (across, sib, diag)[kind]
        return pltpu.make_async_remote_copy(
            src_ref=att.at[slot, rows], dst_ref=att.at[slot, rows],
            send_sem=att_send.at[kind, frame], recv_sem=att_recv.at[kind, frame],
            device_id={"chan": across if kind == 0 else sib}, device_id_type=MESH,
        )

    def pair_at(step):
        return lax.rem(step + pairs - 1, pairs)

    for parts in ((0, 1), (2, 3)):
        @pl.loop(0, pairs)
        def _(step, parts=parts):
            for part in parts:
                token_copy(0, pair_at(step), part).start()
                token_copy(1, pair_at(step), part).start()

    wo_copies = []
    for index, other in enumerate((sib, across, diag)):
        copy = pltpu.make_async_remote_copy(
            src_ref=w_out.at[:, pl.ds(pl.multiple_of(other * width, width), width)],
            dst_ref=wo.at[me], send_sem=wo_send.at[index], recv_sem=wo_recv.at[index],
            device_id={"chan": other}, device_id_type=MESH,
        )
        copy.start()
        wo_copies.append(copy)

    loads[5].wait()
    channel = lax.broadcasted_iota(jnp.int32, (HDIM, 2 * width), 1)
    inner = lax.broadcasted_iota(jnp.int32, (HDIM, 2 * width), 0)
    same = lax.rem(channel, HDIM) == inner
    spread_k = (same & (channel < width)).astype(f32)
    spread_v = (same & (channel >= width)).astype(f32)
    wide = jnp.dot(pool_kernel[0], spread_k, precision=HIGHEST, preferred_element_type=f32)
    wide = wide + jnp.dot(pool_kernel[1], spread_v, precision=HIGHEST, preferred_element_type=f32)
    column = lax.broadcasted_iota(jnp.int32, (WW, 2 * width), 0)
    place = lax.rem(column, 4)
    for tap in range(9):
        line = jnp.where((place == 3) & (column < WW - 1), wide[3 * tap : 3 * tap + 1], 0.0)
        line = jnp.where(place == 0, wide[3 * tap + 1 : 3 * tap + 2], line)
        line = jnp.where(place == 1, wide[3 * tap + 2 : 3 * tap + 3], line)
        taps[tap] = line
    pre[...] = jnp.zeros_like(pre)

    def slab(slot, first, i):
        total = None
        for second in range(3):
            if i == 0 and second == 0:
                continue
            group, row = (i - 1, 3) if second == 0 else (i, second - 1)
            term = field[slot, group, row] * taps[3 * first + second]
            total = term if total is None else total + term
        return total

    def column_sum(block):
        rows_in = block.shape[0]
        r = lax.broadcasted_iota(jnp.int32, (rows_in // 4, rows_in), 0)
        c = lax.broadcasted_iota(jnp.int32, (rows_in // 4, rows_in), 1)
        pick = ((c >= 4 * r - 1) & (c <= 4 * r + 1)).astype(f32)
        return jnp.dot(pick, block, precision=HIGHEST, preferred_element_type=f32)

    halo = pltpu.make_async_remote_copy(
        src_ref=halo_out, dst_ref=halo_in, send_sem=halo_send, recv_sem=halo_recv,
        device_id={"tm": tm_at(1)}, device_id_type=MESH,
    )

    for load in loads[:4]:
        load.wait()

    def project(pair, parts, columns):
        arrivals = []
        for part in parts:
            token_arrival(0, pair, part).wait_recv()
            token_copy(2, pair, part).start()
        for part in parts:
            token_arrival(1, pair, part).wait_recv()
            token_arrival(2, pair, part).wait_recv()
        total = None
        for s in range(4):
            pieces = [part_of(tok.at[s], pair, part)[...].reshape(-1, width) for part in parts]
            term = jnp.dot(
                jnp.concatenate(pieces, axis=0),
                weights[s * width : (s + 1) * width, :columns],
                preferred_element_type=f32,
            )
            total = term if total is None else total + term
        return total.astype(bf16)

    def project_pooled(pair):
        total = project(pair, (0, 1), 3 * width)
        both = pl.ds(2 * pair, 2)
        queries[both, :, 0:2] = total[:FRAME, :width].reshape(2, 4, 2, WW, width)
        queries[both, 0:3, 3] = total[FRAME:, :width].reshape(2, 3, WW, width)
        field[:, :, 0:2] = total[:FRAME, width:].astype(f32).reshape(2, 4, 2, WW, 2 * width)
        field[:, 0:3, 3] = total[FRAME:, width:].astype(f32).reshape(2, 3, WW, 2 * width)
        for i in range(HH // 4):
            pre[pair, i] = pre[pair, i] + slab(0, 1, i) + slab(1, 2, i)
            pre[pair + 1, i] = pre[pair + 1, i] + slab(1, 0, i)

    g0 = lax.broadcasted_iota(jnp.int32, (width, width), 0) // HDIM
    g1 = lax.broadcasted_iota(jnp.int32, (width, width), 1) // HDIM
    averaging = jnp.where(g0 == g1, 1.0 / HDIM, 0.0).astype(f32)
    half = pairs // 2
    halo_rows = HH // 4 * (WW // 4)
    half_rows = half * halo_rows

    def normalise(phase):
        pooled = column_sum(
            pre[phase * half : (phase + 1) * half].reshape(half * HH // 4 * WW, 2 * width)
        )
        if phase == 0:
            pooled = jnp.concatenate([pooled[:halo_rows] + halo_in[...], pooled[halo_rows:]], axis=0)
        for part in range(2):
            x = pooled[:, part * width : (part + 1) * width]
            center = x - jnp.dot(x, averaging, precision=HIGHEST, preferred_element_type=f32)
            spread = jnp.dot(
                center * center, averaging, precision=HIGHEST, preferred_element_type=f32
            )
            gathered[tm, phase, :, part * width : (part + 1) * width] = (
                center * lax.rsqrt(spread + EPSILON)
            ).astype(bf16)

    def block_copy(index, source, target, phase):
        return pltpu.make_async_remote_copy(
            src_ref=gathered.at[source, phase], dst_ref=gathered.at[source, phase],
            send_sem=gat_send.at[index, phase], recv_sem=gat_recv.at[source, phase],
            device_id={"tm": target}, device_id_type=MESH,
        )

    sends = []

    def send_block(phase):
        if relayed:
            targets = [tm_at(2), tm_at(6), tm_at(4), beside]
        else:
            targets = [tm_at(d) for d in offsets]
        for index, target in enumerate(targets):
            copy = block_copy(index, tm, target, phase)
            copy.start()
            sends.append(copy)

    def relay_block(phase):
        if not relayed:
            return
        for index, d in enumerate((2, 6, 4)):
            copy = block_copy(4 + index, tm_at(d), beside, phase)
            copy.wait_recv()
            copy.start()
            sends.append(copy)

    lane_head = lax.broadcasted_iota(jnp.int32, (half_rows, width), 1) // HDIM

    def spread_block(place, slot, phase):
        start = (2 * place + phase) * half_rows
        rows = slice(start, start + half_rows)
        keys = gathered[slot, phase, :, :width]
        values = gathered[slot, phase, :, width:]
        for h in range(heads):
            k_big[h, rows, :] = keys * jnp.where(lane_head == h, HDIM**-0.5, 0.0).astype(bf16)
            v_big[h, rows, :] = values * jnp.where(lane_head == h, 1.0, 0.0).astype(bf16)

    def spread_blocks(phase):
        spread_block(0, tm, phase)
        if relayed:
            for place, d in enumerate((2, 6)):
                spread_block(1 + place, tm_at(d), phase)
            others = [beside] + [lax.rem(beside + d, n_tm) for d in (2, 6, 4)]
            first = 3
        else:
            others = [tm_at(d) for d in offsets]
            first = 1
        for place, slot in enumerate(others):
            block_copy(0, slot, beside, phase).wait_recv()
            spread_block(first + place, slot, phase)

    project_pooled(pairs - 1)
    halo_out[...] = column_sum(pre[pairs].reshape(HH // 4 * WW, 2 * width))
    halo.start()

    @pl.loop(1, pairs - 1)
    def _(step):
        project_pooled(pair_at(step))

    halo.wait_recv()
    normalise(0)
    send_block(0)
    relay_block(0)
    project_pooled(pairs - 2)
    normalise(1)
    send_block(1)
    spread_blocks(0)
    relay_block(1)

    @pl.loop(0, pairs)
    def _(step):
        pair = pair_at(step)
        total = project(pair, (2, 3), width)
        both = pl.ds(2 * pair, 2)
        queries[both, :, 2] = total[: FRAME // 2].reshape(2, 4, WW, width)
        queries[both, 3, 3] = total[FRAME // 2 :].reshape(2, WW, width)

    spread_blocks(1)

    out_head = lax.broadcasted_iota(jnp.int32, (FRAME, width), 1) // HDIM

    @pl.loop(0, frames)
    def _(frame):
        rows = rows_of(frame)
        q = queries[frame].reshape(FRAME, width)
        blended = None
        divisor = None
        for h in range(heads):
            scores = lax.dot_general(
                q, k_big[h], (((1,), (1,)), ((), ())), preferred_element_type=f32
            )
            weighted = jnp.exp(scores - jnp.max(scores, axis=-1, keepdims=True))
            summed = jnp.sum(weighted, axis=-1, keepdims=True)
            term = jnp.dot(weighted.astype(bf16), v_big[h], preferred_element_type=f32)
            blended = term if blended is None else blended + term
            wide_sum = jnp.broadcast_to(summed, (FRAME, width))
            divisor = wide_sum if divisor is None else jnp.where(out_head == h, wide_sum, divisor)
        att[me, rows] = (blended / divisor + q.astype(f32)).astype(bf16)
        att_copy(0, frame).start()
        att_copy(1, frame).start()

    loads[4].wait()
    for index, other in enumerate((sib, across, diag)):
        pltpu.make_async_remote_copy(
            src_ref=wo.at[other], dst_ref=wo.at[other],
            send_sem=wo_send.at[index], recv_sem=wo_recv.at[index],
            device_id={"chan": other}, device_id_type=MESH,
        ).wait_recv()

    @pl.loop(0, frames)
    def _(frame):
        rows = rows_of(frame)
        att_arrival(0, frame).wait_recv()
        att_copy(2, frame).start()
        att_arrival(1, frame).wait_recv()
        att_arrival(2, frame).wait_recv()
        total = tok[me, frame].reshape(FRAME, width).astype(f32)
        for s in range(4):
            total = total + jnp.dot(att[s, rows], wo[s], preferred_element_type=f32)
        out[rows, :] = total.astype(bf16)

    @pl.loop(0, frames)
    def _(frame):
        for kind in range(3):
            att_copy(kind, frame).wait_send()

    @pl.loop(0, pairs)
    def _(pair):
        for kind in range(3):
            for part in range(4):
                token_copy(kind, pair, part).wait_send()

    for copy in wo_copies + sends + [halo]:
        copy.wait_send()


def per_device(n_tm, n_chan, tokens, w_query, w_key, w_value, w_out, pool_kernel):
    rows, width = tokens.shape
    frames = rows // FRAME
    pairs = frames // 2
    block = pairs * (HH // 4) * (WW // 4)
    reach = min(6, (n_tm - 1) // 2)
    spans = 2 * reach + 1
    heads = width // HDIM
    dma = pltpu.SemaphoreType.DMA
    anywhere = pl.BlockSpec(memory_space=pltpu.HBM)
    vmem = pl.BlockSpec(memory_space=pltpu.VMEM)
    return pl.pallas_call(
        functools.partial(kernel, n_tm, reach, frames, width),
        out_shape=jax.ShapeDtypeStruct((rows, width), bf16),
        in_specs=[anywhere] * 6,
        out_specs=vmem,
        scratch_shapes=[
            pltpu.VMEM(pool_kernel.shape, f32),
            pltpu.VMEM((n_chan, frames, HH // 4, 4, WW, width), bf16),
            pltpu.VMEM((D, 3 * width), bf16),
            pltpu.VMEM((n_chan, width, width), bf16),
            pltpu.VMEM((frames, HH // 4, 4, WW, width), bf16),
            pltpu.VMEM((2, HH // 4, 4, WW, 2 * width), f32),
            pltpu.VMEM((9, WW, 2 * width), f32),
            pltpu.VMEM((pairs + 1, HH // 4, WW, 2 * width), f32),
            pltpu.VMEM((HH // 4 * (WW // 4), 2 * width), f32),
            pltpu.VMEM((HH // 4 * (WW // 4), 2 * width), f32),
            pltpu.VMEM((n_tm, 2, block // 2, 2 * width), bf16),
            pltpu.VMEM((heads, spans * block, width), bf16),
            pltpu.VMEM((heads, spans * block, width), bf16),
            pltpu.VMEM((n_chan, rows, width), bf16),
            dma((6,)),
            dma((3, pairs, 4)),
            dma((3, pairs, 4)),
            dma((3,)),
            dma((3,)),
            dma,
            dma,
            dma((max(7, 2 * reach), 2)),
            dma((n_tm, 2)),
            dma((3, frames)),
            dma((3, frames)),
        ],
        compiler_params=pltpu.CompilerParams(
            collective_id=0, has_side_effects=True, vmem_limit_bytes=63 * 1024 * 1024
        ),
    )(tokens.reshape(frames, HH // 4, 4, WW, width), w_query, w_key, w_value, w_out, pool_kernel)


def solution(mesh):
    shape = dict(mesh.shape)
    return jax.shard_map(
        functools.partial(per_device, shape["tm"], shape["chan"]),
        mesh=mesh,
        in_specs=(
            P("tm", "chan"),
            P(None, "chan"),
            P(None, "chan"),
            P(None, "chan"),
            P("chan", None),
            P(),
        ),
        out_specs=P("tm", "chan"),
        check_vma=False,
    )
```

time: 79.2 us -> 73.3 us (0.926)
  local copies, waits for them, and re-layouts: 7.11 us -> 3.62 us
  Pallas kernels: 71.6 us -> 68.7 us
    unnamed x12 -> x2, local copies, waits for them, and re-layouts: 7.11 us -> 3.62 us
    pallas_call x1, Pallas kernels: 71.6 us -> 68.7 us  [per_device(): pl.pallas_call(functools.partial(kernel, n_tm, reach, frames, width), out...]
where the time goes in v2:
time: 73.3 us; the launch traced here: 72.3 us
  Pallas kernels  68.7 us (94%)
  local copies, waits for them, and re-layouts  3.62 us (5%)
    pallas_call x1, Pallas kernels, per_device(): pl.pallas_call(functools.partial(kernel, n_tm, reach, frames, width), out...  68.7 us
    unnamed x2, local copies, waits for them, and re-layouts  3.62 us

profile of v2, /device:TPU:3, one launch (start us, length us, event | category | flops | bytes accessed | tf_op | source)
XLA Modules:
  0.0 72.3 jit_solution(14482545048595852076)
XLA Ops:
  0.0 1.4 %copy.7.pool_hbm = f32[2,27,64]{2,1,0:T(8,128)} copy(f32[2,27,64]{2,0,1:T(2,128)} %param.11) | data formatting | bytes 27648 | tf_op args[5]
  1.4 68.7 %shard_map.64 = bf16[2048,256]{1,0:T(8,128)(2,1)} custom-call(bf16[8,4,4,16,256]{4,3,2,1,0:T(8,128)(2,1)} %bitcast.1, bf16[1024,256]{1,0:T(8,128)(2,1)} %w_query.1, bf16[1024,256]{1,0:T(8,128)(2,1)} %w_key.1, bf16[1024,256]{1,0:T(8,128)(2,1)} %w_value.1, bf16[256,1024]{1,0:T(8,128)(2,1)} %w_out.1, f32[2,27,64]{2,1,0:T(8,128)} %copy.7.pool_hbm), custom_call_target="tpu_custom_call" | custom-call | tf_op jit(solution)/shard_map/pallas_call | solution.py:378
  70.0 2.3 %copy.9 = bf16[2048,256]{1,0:T(8,128)(2,1)} copy(bf16[2048,256]{1,0:T(8,128)(2,1)} %shard_map.64) | data formatting | bytes 2097152

commit v3 on v2

--- a/solution.py
+++ b/solution.py
@@ -48,11 +48,13 @@
         pltpu.make_async_copy(w_query, weights.at[:, pl.ds(0, width)], local_sem.at[0]),
         pltpu.make_async_copy(w_key, weights.at[:, pl.ds(width, width)], local_sem.at[1]),
         pltpu.make_async_copy(w_value, weights.at[:, pl.ds(2 * width, width)], local_sem.at[2]),
-        pltpu.make_async_copy(tokens, tok.at[me], local_sem.at[3]),
         pltpu.make_async_copy(
             w_out.at[:, pl.ds(pl.multiple_of(me * width, width), width)], wo.at[me], local_sem.at[4]
         ),
-        pltpu.make_async_copy(pool_hbm, pool_kernel, local_sem.at[5]),
+        pltpu.make_async_copy(pool_hbm, pool_kernel, local_sem.at[3]),
+    ] + [
+        pltpu.make_async_copy(tokens.at[:, :, :, row], tok.at[me, :, kept], local_sem.at[5 + kept])
+        for kept, row in enumerate((0, 1, 3, 2))
     ]
     for load in loads:
         load.start()
@@ -65,20 +67,13 @@
     pl.semaphore_wait(barrier, 3 + len(offsets))
 
     def part_of(ref, pair, part):
-        both = pl.ds(2 * pair, 2)
-        if part == 0:
-            return ref.at[both, :, pl.ds(0, 2)]
-        if part == 1:
-            return ref.at[both, pl.ds(0, 3), 3]
-        if part == 2:
-            return ref.at[both, :, 2]
-        return ref.at[both, 3, 3]
+        return ref.at[pair, pl.ds(0, 3)] if part == 0 else ref.at[pair, 3]
 
     def token_copy(kind, pair, part):
         if kind == 2:
             source, slot = part_of(tok.at[across], pair, part), across
         else:
-            source, slot = part_of(tokens, pair, part), me
+            source, slot = part_of(tok.at[me], pair, part), me
         return pltpu.make_async_remote_copy(
             src_ref=source, dst_ref=part_of(tok.at[slot], pair, part),
             send_sem=tok_send.at[kind, pair, part], recv_sem=tok_recv.at[kind, pair, part],
@@ -114,7 +109,9 @@
     def pair_at(step):
         return lax.rem(step + pairs - 1, pairs)
 
-    for parts in ((0, 1), (2, 3)):
+    for load in loads[5:]:
+        load.wait()
+    for parts in ((0,), (1,)):
         @pl.loop(0, pairs)
         def _(step, parts=parts):
             for part in parts:
@@ -131,7 +128,7 @@
         copy.start()
         wo_copies.append(copy)
 
-    loads[5].wait()
+    loads[4].wait()
     channel = lax.broadcasted_iota(jnp.int32, (HDIM, 2 * width), 1)
     inner = lax.broadcasted_iota(jnp.int32, (HDIM, 2 * width), 0)
     same = lax.rem(channel, HDIM) == inner
@@ -170,7 +167,7 @@
         device_id={"tm": tm_at(1)}, device_id_type=MESH,
     )
 
-    for load in loads[:4]:
+    for load in loads[:3]:
         load.wait()
 
     def project(pair, parts, columns):
@@ -193,12 +190,12 @@
         return total.astype(bf16)
 
     def project_pooled(pair):
-        total = project(pair, (0, 1), 3 * width)
+        total = project(pair, (0,), 3 * width)
         both = pl.ds(2 * pair, 2)
-        queries[both, :, 0:2] = total[:FRAME, :width].reshape(2, 4, 2, WW, width)
-        queries[both, 0:3, 3] = total[FRAME:, :width].reshape(2, 3, WW, width)
-        field[:, :, 0:2] = total[:FRAME, width:].astype(f32).reshape(2, 4, 2, WW, 2 * width)
-        field[:, 0:3, 3] = total[FRAME:, width:].astype(f32).reshape(2, 3, WW, 2 * width)
+        for kept, row in enumerate((0, 1, 3)):
+            block = total[kept * FRAME // 2 : (kept + 1) * FRAME // 2]
+            queries[both, :, row] = block[:, :width].reshape(2, 4, WW, width)
+            field[:, :, row] = block[:, width:].astype(f32).reshape(2, 4, WW, 2 * width)
         for i in range(HH // 4):
             pre[pair, i] = pre[pair, i] + slab(0, 1, i) + slab(1, 2, i)
             pre[pair + 1, i] = pre[pair + 1, i] + slab(1, 0, i)
@@ -300,10 +297,9 @@
     @pl.loop(0, pairs)
     def _(step):
         pair = pair_at(step)
-        total = project(pair, (2, 3), width)
+        total = project(pair, (1,), width)
         both = pl.ds(2 * pair, 2)
-        queries[both, :, 2] = total[: FRAME // 2].reshape(2, 4, WW, width)
-        queries[both, 3, 3] = total[FRAME // 2 :].reshape(2, WW, width)
+        queries[both, :, 2] = total.reshape(2, 4, WW, width)
 
     spread_blocks(1)
 
@@ -329,7 +325,7 @@
         att_copy(0, frame).start()
         att_copy(1, frame).start()
 
-    loads[4].wait()
+    loads[3].wait()
     for index, other in enumerate((sib, across, diag)):
         pltpu.make_async_remote_copy(
             src_ref=wo.at[other], dst_ref=wo.at[other],
@@ -344,7 +340,8 @@
         att_copy(2, frame).start()
         att_arrival(1, frame).wait_recv()
         att_arrival(2, frame).wait_recv()
-        total = tok[me, frame].reshape(FRAME, width).astype(f32)
+        own = [tok[me, frame // 2, kept, lax.rem(frame, 2)] for kept in (0, 1, 3, 2)]
+        total = jnp.stack(own, axis=1).reshape(FRAME, width).astype(f32)
         for s in range(4):
             total = total + jnp.dot(att[s, rows], wo[s], preferred_element_type=f32)
         out[rows, :] = total.astype(bf16)
@@ -357,7 +354,7 @@
     @pl.loop(0, pairs)
     def _(pair):
         for kind in range(3):
-            for part in range(4):
+            for part in range(2):
                 token_copy(kind, pair, part).wait_send()
 
     for copy in wo_copies + sends + [halo]:
@@ -382,7 +379,7 @@
         out_specs=vmem,
         scratch_shapes=[
             pltpu.VMEM(pool_kernel.shape, f32),
-            pltpu.VMEM((n_chan, frames, HH // 4, 4, WW, width), bf16),
+            pltpu.VMEM((n_chan, pairs, 4, 2, HH // 4, WW, width), bf16),
             pltpu.VMEM((D, 3 * width), bf16),
             pltpu.VMEM((n_chan, width, width), bf16),
             pltpu.VMEM((frames, HH // 4, 4, WW, width), bf16),
@@ -395,9 +392,9 @@
             pltpu.VMEM((heads, spans * block, width), bf16),
             pltpu.VMEM((heads, spans * block, width), bf16),
             pltpu.VMEM((n_chan, rows, width), bf16),
-            dma((6,)),
-            dma((3, pairs, 4)),
-            dma((3, pairs, 4)),
+            dma((9,)),
+            dma((3, pairs, 2)),
+            dma((3, pairs, 2)),
             dma((3,)),
             dma((3,)),
             dma,
@@ -410,7 +407,7 @@
         compiler_params=pltpu.CompilerParams(
             collective_id=0, has_side_effects=True, vmem_limit_bytes=63 * 1024 * 1024
         ),
-    )(tokens.reshape(frames, HH // 4, 4, WW, width), w_query, w_key, w_value, w_out, pool_kernel)
+    )(tokens.reshape(pairs, 2, HH // 4, 4, WW, width), w_query, w_key, w_value, w_out, pool_kernel)
 
 
 def solution(mesh):

time: 73.3 us -> 73.2 us (level)
  no operation moved by 1% of the time
where the time goes in v3:
time: 73.2 us; the launch traced here: 72 us
  Pallas kernels  68.4 us (93%)
  local copies, waits for them, and re-layouts  3.62 us (5%)
    pallas_call x1, Pallas kernels, per_device(): pl.pallas_call(functools.partial(kernel, n_tm, reach, frames, width), out...  68.4 us
    unnamed x2, local copies, waits for them, and re-layouts  3.62 us

profile of v3, /device:TPU:3, one launch (start us, length us, event | category | flops | bytes accessed | tf_op | source)
XLA Modules:
  0.0 72.0 jit_solution(11172315119025521205)
XLA Ops:
  0.0 1.4 %copy.7.pool_hbm = f32[2,27,64]{2,1,0:T(8,128)} copy(f32[2,27,64]{2,0,1:T(2,128)} %param.11) | data formatting | bytes 27648 | tf_op args[5]
  1.4 68.4 %shard_map.64 = bf16[2048,256]{1,0:T(8,128)(2,1)} custom-call(bf16[4,2,4,4,16,256]{5,4,3,2,1,0:T(8,128)(2,1)} %bitcast.1, bf16[1024,256]{1,0:T(8,128)(2,1)} %w_query.1, bf16[1024,256]{1,0:T(8,128)(2,1)} %w_key.1, bf16[1024,256]{1,0:T(8,128)(2,1)} %w_value.1, bf16[256,1024]{1,0:T(8,128)(2,1)} %w_out.1, f32[2,27,64]{2,1,0:T(8,128)} %copy.7.pool_hbm), custom_call_target="tpu_custom_call" | custom-call | tf_op jit(solution)/shard_map/pallas_call | solution.py:375
  69.8 2.3 %copy.9 = bf16[2048,256]{1,0:T(8,128)(2,1)} copy(bf16[2048,256]{1,0:T(8,128)(2,1)} %shard_map.64) | data formatting | bytes 2097152

commit v4 on v3

--- a/solution.py
+++ b/solution.py
@@ -116,7 +116,11 @@
         def _(step, parts=parts):
             for part in parts:
                 token_copy(0, pair_at(step), part).start()
-                token_copy(1, pair_at(step), part).start()
+
+    for part in range(2):
+        @pl.loop(0, pairs)
+        def _(step, part=part):
+            token_copy(1, pair_at(step), part).start()
 
     wo_copies = []
     for index, other in enumerate((sib, across, diag)):

time: 73.2 us -> 73.2 us (level)
  no operation moved by 1% of the time
where the time goes in v4:
time: 73.2 us; the launch traced here: 72 us
  Pallas kernels  68.4 us (93%)
  local copies, waits for them, and re-layouts  3.62 us (5%)
    pallas_call x1, Pallas kernels, per_device(): pl.pallas_call(functools.partial(kernel, n_tm, reach, frames, width), out...  68.4 us
    unnamed x2, local copies, waits for them, and re-layouts  3.62 us

profile of v4, /device:TPU:3, one launch (start us, length us, event | category | flops | bytes accessed | tf_op | source)
XLA Modules:
  0.0 72.0 jit_solution(1943785081930183749)
XLA Ops:
  0.0 1.4 %copy.7.pool_hbm = f32[2,27,64]{2,1,0:T(8,128)} copy(f32[2,27,64]{2,0,1:T(2,128)} %param.11) | data formatting | bytes 27648 | tf_op args[5]
  1.4 68.4 %shard_map.64 = bf16[2048,256]{1,0:T(8,128)(2,1)} custom-call(bf16[4,2,4,4,16,256]{5,4,3,2,1,0:T(8,128)(2,1)} %bitcast.1, bf16[1024,256]{1,0:T(8,128)(2,1)} %w_query.1, bf16[1024,256]{1,0:T(8,128)(2,1)} %w_key.1, bf16[1024,256]{1,0:T(8,128)(2,1)} %w_value.1, bf16[256,1024]{1,0:T(8,128)(2,1)} %w_out.1, f32[2,27,64]{2,1,0:T(8,128)} %copy.7.pool_hbm), custom_call_target="tpu_custom_call" | custom-call | tf_op jit(solution)/shard_map/pallas_call | solution.py:379
  69.8 2.3 %copy.9 = bf16[2048,256]{1,0:T(8,128)(2,1)} copy(bf16[2048,256]{1,0:T(8,128)(2,1)} %shard_map.64) | data formatting | bytes 2097152
